TPU v7x, 256 devices: a whole 4x4x8 slice. The times are simulated.
256 devices in a mesh: item: 64 (over z, y, core), dp: 4 (over x).
Axes of the slice: x: 4, y: 4, z: 8, core: 2. Of those that a mesh axis runs over, the one named last changes fastest.
Arguments:
- query_feats: bfloat16 [4, 1024, 256], P('dp', 'item'), may hold values from -6 to 6
- positives: int32 [4, 1024], P('dp'), may hold values from 0 to 262143
- query_count: int32 [4, 64], P('dp'), may hold values from 1 to 16, as said below
- item_table: bfloat16 [262144, 256], P('item'), may hold values from -6 to 6
- item_gates: float32 [4, 262144], P(None, 'item'), may hold values from -5 to 5
- w_in: bfloat16 [256, 512], replicated, may hold values from -0.375 to 0.375
- w_out: bfloat16 [512, 256], replicated, may hold values from -0.25 to 0.25
- w_gate: bfloat16 [512, 4], replicated, may hold values from -1.25 to 1.25
Outputs:
- grad_feats: float32 [4, 1024, 256], P('dp', 'item')
- grad_w_in: float32 [256, 512], replicated
- grad_w_out: float32 [512, 256], replicated
- grad_w_gate: float32 [512, 4], replicated
Inputs may be any that keep to these rules, and one draw needn't show every extreme that they name: `query_count`: valid queries of a device's slots; the counts of one group sum to at most 768, exactly that in some group, and some device of every group has all 16 slots valid.
All inputs are finite; a program needn't handle non-finite values.
Results may differ from a plain program's by a relative error of at most 0.0053.
Values may be sent and summed in bfloat16 or wider, within the bound.
A program may use at most 64 MiB of HBM per device.

v0:
```python
import jax
import jax.numpy as jnp
from jax import lax
from jax.sharding import PartitionSpec as P

EPS = 1e-06
TAU = 0.05


def unit_rows(raw_vals):
    scale = lax.rsqrt(jnp.sum(raw_vals * raw_vals, axis=-1, keepdims=True) + EPS)
    return (raw_vals * scale, scale)


def gate_weights(gate_logits, reduce_axis):
    exp_terms = jnp.exp(gate_logits)
    return exp_terms / jnp.sum(exp_terms, axis=reduce_axis, keepdims=True)


def item_sweep(query_rows, query_gate, item_norm, item_gates):
    row_count = query_rows.shape[0]
    components = query_rows.shape[1]
    comp_width = query_rows.shape[2]
    item_span = item_norm.shape[0]
    block_len = min(512, item_span)
    block_count = item_span // block_len
    item_blocks = item_norm.reshape(block_count, block_len, components, comp_width)
    gate_blocks = item_gates.reshape(components, block_count, block_len).transpose(1, 0, 2)
    gate_f = query_gate.astype(jnp.float32).T[:, :, None]

    def one_block(state_in, input_block_part):
        totals, update_delta, gate_sum = state_in
        item_part, gate_part = input_block_part
        score_matrix = jnp.einsum(
            "rkd,ikd->kri", query_rows, item_part, preferred_element_type=jnp.float32
        )
        weights = gate_weights(gate_f + gate_part[:, None, :], 0)
        logits = jnp.sum(weights * score_matrix, axis=0) / TAU
        exp_logit = jnp.exp(logits)
        totals = totals + jnp.sum(exp_logit, axis=1)
        coef_bf = (exp_logit[None] * weights / TAU).astype(jnp.bfloat16)
        update_delta = update_delta + jnp.einsum(
            "kri,ikd->rkd", coef_bf, item_part, preferred_element_type=jnp.float32
        )
        gate_sum = (
            gate_sum
            + jnp.sum(exp_logit[None] * weights * (score_matrix - TAU * logits[None]), axis=2) / TAU
        )
        return ((totals, update_delta, gate_sum), None)

    initial = (
        jnp.zeros((row_count,), jnp.float32),
        jnp.zeros((row_count, components, comp_width), jnp.float32),
        jnp.zeros((components, row_count), jnp.float32),
    )
    (totals, update_delta, gate_sum), _ = lax.scan(one_block, initial, (item_blocks, gate_blocks))
    return (totals, update_delta, gate_sum.T)


def positive_terms(query_rows, query_gate, positive, item_norm, item_gates, item_base):
    item_span = item_norm.shape[0]
    local_id = positive - item_base
    inside = (local_id >= 0) & (local_id < item_span)
    safe_id = jnp.clip(local_id, 0, item_span - 1)
    item_pos = jnp.take(item_norm, safe_id, axis=0).astype(jnp.float32)
    gate_pos = jnp.take(item_gates, safe_id, axis=1).T
    query_float_rows = query_rows.astype(jnp.float32)
    score_pos = jnp.sum(query_float_rows * item_pos, axis=-1)
    weight_pos = gate_weights(query_gate.astype(jnp.float32) + gate_pos, 1)
    logit_pos = jnp.sum(weight_pos * score_pos, axis=-1) / TAU
    keep_rows = inside.astype(jnp.float32)
    pos_query = weight_pos[:, :, None] * item_pos / TAU * keep_rows[:, None, None]
    pos_gate = weight_pos * (score_pos - TAU * logit_pos[:, None]) / TAU * keep_rows[:, None]
    return (pos_query, pos_gate)


def per_device(query_feats, positives, query_count, item_table, item_gates, w_in, w_out, w_gate):
    shard_count = lax.axis_size("item")
    item_rank = lax.axis_index("item")
    own_rows = query_feats.shape[1]
    feat_width = query_feats.shape[2]
    components = w_gate.shape[1]
    emb_width = w_out.shape[1]
    comp_width = emb_width // components
    slot_total = own_rows * shard_count
    features = query_feats[0]
    counts = query_count[0]
    preact = jnp.dot(features, w_in, preferred_element_type=jnp.float32)
    hidden = jax.nn.silu(preact).astype(jnp.bfloat16)
    query_raw = jnp.dot(hidden, w_out, preferred_element_type=jnp.float32).reshape(
        own_rows, components, comp_width
    )
    query_gate = jnp.dot(hidden, w_gate, preferred_element_type=jnp.float32).astype(jnp.bfloat16)
    query_unit, query_scale = unit_rows(query_raw)
    query_norm = query_unit.astype(jnp.bfloat16).reshape(own_rows, emb_width)
    all_query, all_gate = (
        lax.all_gather(query_norm, "item", axis=0, tiled=True),
        lax.all_gather(query_gate, "item", axis=0, tiled=True),
    )
    item_span = item_table.shape[0]
    item_norm = unit_rows(
        item_table.astype(jnp.float32).reshape(item_span, components, comp_width)
    )[0].astype(jnp.bfloat16)
    slot_in_dev = jnp.arange(own_rows, dtype=jnp.int32)
    valid_slot = (slot_in_dev[None, :] < counts[:, None]).reshape(slot_total)
    item_base = item_rank * item_span
    group_position = positives[0]
    query_rows = all_query.reshape(-1, components, comp_width)
    totals, update_delta, gate_sum = item_sweep(query_rows, all_gate, item_norm, item_gates)
    pos_query, pos_gate = positive_terms(
        query_rows, all_gate, group_position, item_norm, item_gates, item_base
    )
    live_f = valid_slot.astype(jnp.float32)
    totals_all = lax.psum(totals, "item")
    query_term_part = (update_delta / totals_all[:, None, None] - pos_query) * live_f[:, None, None]
    term_gate = (gate_sum / totals_all[:, None] - pos_gate) * live_f[:, None]
    grad_query, grad_gate = (
        lax.psum_scatter(
            query_term_part.reshape(slot_total, emb_width), "item", scatter_dimension=0, tiled=True
        ),
        lax.psum_scatter(term_gate, "item", scatter_dimension=0, tiled=True),
    )
    grad_query = grad_query.reshape(own_rows, components, comp_width)
    dot_sum = jnp.sum(grad_query * query_raw, axis=-1, keepdims=True)
    grad_raw = (query_scale * grad_query - query_raw * query_scale**3 * dot_sum).reshape(
        own_rows, emb_width
    )
    highest = lax.Precision.HIGHEST
    grad_hidden = jnp.dot(grad_raw, w_out.astype(jnp.float32).T, precision=highest) + jnp.dot(
        grad_gate, w_gate.astype(jnp.float32).T, precision=highest
    )
    sigmoid_pre = jax.nn.sigmoid(preact)
    grad_preact = grad_hidden * sigmoid_pre * (1.0 + preact * (1.0 - sigmoid_pre))
    grad_feats = jnp.dot(grad_preact, w_in.astype(jnp.float32).T, precision=highest).reshape(
        1, own_rows, feat_width
    )
    hidden_f = hidden.astype(jnp.float32)
    part_in = jnp.dot(features.astype(jnp.float32).T, grad_preact, precision=highest)
    part_out = jnp.dot(hidden_f.T, grad_raw, precision=highest)
    part_gate = jnp.dot(hidden_f.T, grad_gate, precision=highest)
    grad_w_in, grad_w_out, grad_w_gate = lax.psum((part_in, part_out, part_gate), ("item", "dp"))
    return (grad_feats, grad_w_in, grad_w_out, grad_w_gate)


def solution(mesh):
    in_specs = (
        P("dp", "item", None),
        P("dp", None),
        P("dp", None),
        P("item", None),
        P(None, "item"),
        P(),
        P(),
        P(),
    )
    out_specs = (P("dp", "item", None), P(), P(), P())
    return jax.shard_map(
        per_device, mesh=mesh, in_specs=in_specs, out_specs=out_specs, check_vma=False
    )
```

profile of v0, /device:TPU:2, one launch (start us, length us, event | category | flops | bytes accessed | tf_op | source)
XLA Modules:
  0.0 914.7 jit_solution(16929554966947675786)
XLA Ops:
  16.9 53.5 %all_gather.7 = bf16[1024,256]{1,0:T(8,128)(2,1)S(1)} all-gather(bf16[16,256]{1,0:T(8,128)(2,1)S(1)} %multiply_convert_fusion.9), channel_id=1, replica_groups=mesh['item'=64,'dp'=4] {'item'}, dimensions={0}, use_global_device_ids=true | all-gather | bytes 532480 | tf_op jit(solution)/shard_map/all_gather | solution.py:97
  73.4 7.0 copy.75
  80.4 5.7 gather_fusion.1
  87.5 42.9 %all-gather = bf16[64,16,4]{1,2,0:T(4,128)(2,1)S(1)} all-gather(bf16[1,16,4]{1,2,0:T(4,128)(2,1)S(1)} %fusion.19), channel_id=1, replica_groups=mesh['item'=64,'dp'=4] {'item'}, dimensions={0}, use_global_device_ids=true | all-gather | bytes 8320 | tf_op jit(solution)/shard_map/all_gather | solution.py:98
  132.1 4.4 gather_fusion
  137.7 6.0 copy.81
  147.2 118.4 %while.17 = (s32[]{:T(128)}, f32[1024]{0:T(1024)S(1)}, f32[1024,4,64]{0,2,1:T(8,128)}, f32[4,1024]{1,0:T(4,128)S(1)}, f32[4,1024,1]{1,0,2:T(4,128)S(1)}, /*index...) while((s32[]{:T(128)}, f32[1024]{0:T(1024)S(1)}, ...), condition=%wide.region_7.8_spmd.clone, body=%wide.region_2.7_spmd.clone.sunk | while | flops 573056000 | bytes 49480844 | solution.py:56
  149.4 4.1 fusion.63
  153.8 3.0 fusion.65
  156.8 5.0 fusion.64
  164.0 4.1 fusion.63
  168.4 3.0 fusion.65
  171.4 5.3 fusion.64
  178.8 4.1 fusion.63
  183.2 3.0 fusion.65
  186.2 5.3 fusion.64
  193.6 4.1 fusion.63
  198.0 3.0 fusion.65
  201.1 5.3 fusion.64
  208.4 4.1 fusion.63
  212.9 3.0 fusion.65
  215.9 5.3 fusion.64
  223.3 4.1 fusion.63
  230.7 5.3 fusion.64
  238.1 4.1 fusion.63
  245.5 5.3 fusion.64
  252.9 4.1 fusion.63
  260.4 5.3 fusion.64
  265.7 126.8 %psum.28 = f32[1024]{0:T(1024)S(1)} all-reduce(f32[1024]{0:T(1024)S(1)} %get-tuple-element.108), channel_id=1, replica_groups=mesh['item'=64,'dp'=4] {'item'}, use_global_device_ids=true, to_apply=%region_8.9 | all-reduce | flops 1024 | bytes 8192 | tf_op jit(solution)/shard_map/psum | solution.py:114
  398.0 249.1 %all-reduce = f32[1024,4]{1,0:T(8,128)S(1)} all-reduce(f32[1024,4]{1,0:T(8,128)S(1)} %copy.78), channel_id=3, replica_groups=mesh['item'=64,'dp'=4] {'item'}, use_global_device_ids=true, to_apply=%region_14.15.clone | all-reduce | flops 4096 | bytes 32768
  652.1 71.6 %psum.31 = f32[512,4]{0,1:T(4,128)} all-reduce(f32[512,4]{0,1:T(4,128)S(1)} %fusion.30), channel_id=1, replica_groups=mesh['item'=64,'dp'=4] {'item','dp'}, use_global_device_ids=true, to_apply=%region_17.18 | all-reduce | flops 2048 | bytes 16384 | tf_op jit(solution)/shard_map/psum | solution.py:141
  724.6 179.4 %all-reduce.4.cloned.1.call-done = (f32[256,512]{0,1:T(8,128)}, f32[512,256]{1,0:T(8,128)}) async-done(((f32[256,512]{0,1:T(8,128)}, f32[512,256]{1,0:T(8,128)}), (f32[256,512]{0,1:T(8,128)}, f32[512,256]{1,0:T(8,128)})) %all-reduce.4.cloned.1.call-update) | async-done | bytes 1048592 | tf_op jit(solution)/shard_map/psum | solution.py:141
  (161 shorter events, 63.8 us)
Async XLA Ops:
  7.2 7.3 copy-start
  7.2 639.9 %reduce-scatter.2.cloned.1.call-start = ((), (), s32[]{:S(2)}) async-start(), calls=%async_computation.1 | async-start | bytes 1064960 | tf_op jit(solution)/shard_map/reduce_scatter | solution.py:118
  10.2 3.6 copy-start.16
  10.2 4.2 copy-start.11
  10.2 5.0 copy-start.2
  16.3 0.6 copy-start.7
  73.4 13.9 %copy-start.18 = (bf16[512,4]{0,1:T(4,128)(2,1)S(1)}, bf16[512,4]{0,1:T(4,128)(2,1)}, u32[]{:S(2)}) copy-start(bf16[512,4]{0,1:T(4,128)(2,1)} %param.17) | copy-start | bytes 12292
  80.4 7.1 copy-start.10
  137.7 8.9 copy-start.5
  143.7 2.7 copy-start.15
  144.3 2.9 copy-start.4
  147.2 245.3 %copy-start.17 = (s32[1,64]{1,0:T(1,128)S(1)}, s32[1,64]{1,0:T(1,128)}, u32[]{:S(2)}) copy-start(s32[1,64]{1,0:T(1,128)} %param.12) | copy-start | bytes 772
  147.2 245.4 %copy-start.6 = (f32[1024,4]{0,1:T(4,128)S(1)}, f32[1024,4]{0,1:T(4,128)}, u32[]{:S(2)}) copy-start(f32[1024,4]{0,1:T(4,128)} %copy-done.5) | copy-start | bytes 49156
  149.4 4.4 copy-start.1
  163.9 4.4 copy-start.1
  178.8 4.4 copy-start.1
  193.6 4.4 copy-start.1
  208.4 4.4 copy-start.1
  223.3 4.4 copy-start.1
  238.1 4.4 copy-start.1
  252.9 4.4 copy-start.1
  265.6 130.7 %copy-start.9 = (f32[1,1024]{1,0:T(1,128)S(1)}, f32[1,1024]{1,0:T(1,128)}, u32[]{:S(2)}) copy-start(f32[1,1024]{1,0:T(1,128)} %and_select_fusion) | copy-start | bytes 12292
  265.6 130.9 %copy-start.14 = (f32[16,4]{1,0:T(8,128)S(1)}, f32[16,4]{1,0:T(8,128)}, u32[]{:S(2)}) copy-start(f32[16,4]{1,0:T(8,128)} %get-tuple-element.223) | copy-start | bytes 772
  265.7 131.1 %copy-start.20 = (u32[256]{0:T(256)S(1)}, u32[256]{0:T(256)}, u32[]{:S(2)}) copy-start(u32[256]{0:T(256)} %constant.108) | copy-start | bytes 3076
  265.7 382.5 %copy-start.8 = (f32[16,256]{1,0:T(8,128)S(1)}, f32[16,256]{1,0:T(8,128)}, u32[]{:S(2)}) copy-start(f32[16,256]{1,0:T(8,128)} %copy-done.7) | copy-start | bytes 49156
  265.7 383.3 %copy-start.3 = (bf16[512,256]{1,0:T(8,128)(2,1)S(1)}, bf16[512,256]{1,0:T(8,128)(2,1)}, u32[]{:S(2)}) copy-start(bf16[512,256]{1,0:T(8,128)(2,1)} %param.16) | copy-start | bytes 786436
  393.4 257.1 %copy-start.13 = (f32[16,512]{1,0:T(8,128)S(1)}, f32[16,512]{1,0:T(8,128)}, u32[]{:S(2)}) copy-start(f32[16,512]{1,0:T(8,128)} %get-tuple-element.226) | copy-start | bytes 98308
  393.4 257.1 %copy-start.19 = (bf16[512,4]{0,1:T(4,128)(2,1)S(1)}, bf16[512,4]{0,1:T(4,128)(2,1)}, u32[]{:S(2)}) copy-start(bf16[512,4]{0,1:T(4,128)(2,1)} %param.17) | copy-start | bytes 12292
  393.4 257.2 %copy-start.12 = (bf16[1,16,256]{2,1,0:T(8,128)(2,1)S(1)}, bf16[1,16,256]{2,1,0:T(8,128)(2,1)}, u32[]{:S(2)}) copy-start(bf16[1,16,256]{2,1,0:T(8,128)(2,1)} %param.10) | copy-start | bytes 24580
  396.2 507.7 %all-reduce.4.cloned.1.call-start = ((), (), s32[]{:S(2)}) async-start(), calls=%async_computation.2 | async-start | bytes 2097152 | tf_op jit(solution)/shard_map/psum | solution.py:141
Sparse Core Ops, SparseCore 0:
  396.4 134.9 reduce-scatter.1
  652.0 251.9 all-reduce.3
where the time goes:
time: 916 us; the launch traced here: 915 us
  blocking collectives  544 us (59%)
  waiting for transfers between devices  179 us (20%)
  matrix products  79.4 us (9%)
  other arithmetic  51.6 us (6%)
  local copies, waits for them, and re-layouts  45 us (5%)
  between operations  15 us (2%)
    unnamed x1, blocking collectives  249 us
    psum x1, waiting for transfers between devices, per_device(): lax.psum((part_in, part_out, part_gate), ('item', 'dp'))  179 us
    psum x1, blocking collectives, per_device(): totals_all = lax.psum(totals, 'item')  127 us
    psum x1, blocking collectives, per_device(): lax.psum((part_in, part_out, part_gate), ('item', 'dp'))  71.6 us
    all_gather x1, blocking collectives, per_device(): lax.all_gather(query_norm, 'item', axis=0, tiled=True)  53.5 us
    all_gather x1, blocking collectives, per_device(): lax.all_gather(query_gate, 'item', axis=0, tiled=True)  42.9 us
    dot_general x8, matrix products, one_block(): jnp.einsum('kri,ikd->rkd', coef_bf, item_part, preferred_element_type=jnp...  41.9 us
    dot_general x8, matrix products, one_block(): jnp.einsum('rkd,ikd->kri', query_rows, item_part, preferred_element_type=...  32.5 us
  transfers between devices with their start and end apart: 2, of which 1 were waited for; matrix products, arithmetic and copies ran while one was open for 0% of the time, Pallas kernels for 0%

commit v1 on v0

--- a/solution.py
+++ b/solution.py
@@ -138,7 +138,9 @@
     part_in = jnp.dot(features.astype(jnp.float32).T, grad_preact, precision=highest)
     part_out = jnp.dot(hidden_f.T, grad_raw, precision=highest)
     part_gate = jnp.dot(hidden_f.T, grad_gate, precision=highest)
-    grad_w_in, grad_w_out, grad_w_gate = lax.psum((part_in, part_out, part_gate), ("item", "dp"))
+    grad_w_in, grad_w_out, grad_w_gate = lax.psum(
+        lax.psum((part_in, part_out, part_gate), "dp"), "item"
+    )
     return (grad_feats, grad_w_in, grad_w_out, grad_w_gate)
 
 

time: 916 us -> 902 us (0.985)
  waiting for transfers between devices: 179 us -> 99.1 us
  blocking collectives: 544 us -> 610 us
    psum x1 -> x2, waiting for transfers between devices: 179 us -> 99 us  [the longest x1 53.1 us: per_device(): lax.psum(lax.psum((part_in, part_out, part_gate), 'dp'), 'item')]
    psum x1 -> x2, blocking collectives: 71.6 us -> 138 us  [the longest x1 129 us: per_device(): lax.psum(lax.psum((part_in, part_out, part_gate), 'dp'), 'item')]
  transfers between devices with their start and end apart: 2 -> 3, of which waited for: 1 -> 2; matrix products, arithmetic and copies ran while one was open for 0% -> 0% of each run, Pallas kernels for 0% -> 0%
where the time goes in v1:
time: 902 us; the launch traced here: 900 us
  blocking collectives  610 us (68%)
  waiting for transfers between devices  99.1 us (11%)
  matrix products  79.4 us (9%)
  other arithmetic  51.6 us (6%)
  local copies, waits for them, and re-layouts  45 us (5%)
  between operations  14.7 us (2%)
    unnamed x1, blocking collectives  249 us
    psum x1, blocking collectives, per_device(): lax.psum(lax.psum((part_in, part_out, part_gate), 'dp'), 'item')  129 us
    psum x1, blocking collectives, per_device(): totals_all = lax.psum(totals, 'item')  127 us
    all_gather x1, blocking collectives, per_device(): lax.all_gather(query_norm, 'item', axis=0, tiled=True)  53.5 us
    psum x1, waiting for transfers between devices, per_device(): lax.psum(lax.psum((part_in, part_out, part_gate), 'dp'), 'item')  53.1 us
    psum x1, waiting for transfers between devices, per_device(): lax.psum((part_in, part_out, part_gate), 'dp')  45.9 us
    all_gather x1, blocking collectives, per_device(): lax.all_gather(query_gate, 'item', axis=0, tiled=True)  42.9 us
    dot_general x8, matrix products, one_block(): jnp.einsum('kri,ikd->rkd', coef_bf, item_part, preferred_element_type=jnp...  41.9 us
  transfers between devices with their start and end apart: 3, of which 2 were waited for; matrix products, arithmetic and copies ran while one was open for 0% of the time, Pallas kernels for 0%

profile of v1, /device:TPU:2, one launch (start us, length us, event | category | flops | bytes accessed | tf_op | source)
XLA Modules:
  0.0 900.2 jit_solution(4874927433128612118)
XLA Ops:
  16.9 53.5 %all_gather.7 = bf16[1024,256]{1,0:T(8,128)(2,1)S(1)} all-gather(bf16[16,256]{1,0:T(8,128)(2,1)S(1)} %multiply_convert_fusion.9), channel_id=1, replica_groups=mesh['item'=64,'dp'=4] {'item'}, dimensions={0}, use_global_device_ids=true | all-gather | bytes 532480 | tf_op jit(solution)/shard_map/all_gather | solution.py:97
  73.4 7.0 copy.75
  80.4 5.7 gather_fusion.1
  87.5 42.9 %all-gather = bf16[64,16,4]{1,2,0:T(4,128)(2,1)S(1)} all-gather(bf16[1,16,4]{1,2,0:T(4,128)(2,1)S(1)} %fusion.19), channel_id=1, replica_groups=mesh['item'=64,'dp'=4] {'item'}, dimensions={0}, use_global_device_ids=true | all-gather | bytes 8320 | tf_op jit(solution)/shard_map/all_gather | solution.py:98
  132.1 4.4 gather_fusion
  137.7 6.0 copy.81
  147.2 118.4 %while.17 = (s32[]{:T(128)}, f32[1024]{0:T(1024)S(1)}, f32[1024,4,64]{0,2,1:T(8,128)}, f32[4,1024]{1,0:T(4,128)S(1)}, f32[4,1024,1]{1,0,2:T(4,128)S(1)}, /*index...) while((s32[]{:T(128)}, f32[1024]{0:T(1024)S(1)}, ...), condition=%wide.region_7.8_spmd.clone, body=%wide.region_2.7_spmd.clone.sunk | while | flops 573056000 | bytes 49480844 | solution.py:56
  149.4 4.1 fusion.63
  153.8 3.0 fusion.65
  156.8 5.0 fusion.64
  164.0 4.1 fusion.63
  168.4 3.0 fusion.65
  171.4 5.3 fusion.64
  178.8 4.1 fusion.63
  183.2 3.0 fusion.65
  186.2 5.3 fusion.64
  193.6 4.1 fusion.63
  201.1 5.3 fusion.64
  208.4 4.1 fusion.63
  215.9 5.3 fusion.64
  223.3 4.1 fusion.63
  230.7 5.3 fusion.64
  238.1 4.1 fusion.63
  245.5 5.3 fusion.64
  252.9 4.1 fusion.63
  260.4 5.3 fusion.64
  265.7 126.8 %psum.49 = f32[1024]{0:T(1024)S(1)} all-reduce(f32[1024]{0:T(1024)S(1)} %get-tuple-element.108), channel_id=1, replica_groups=mesh['item'=64,'dp'=4] {'item'}, use_global_device_ids=true, to_apply=%region_8.9 | all-reduce | flops 1024 | bytes 8192 | tf_op jit(solution)/shard_map/psum | solution.py:114
  398.0 249.1 %all-reduce = f32[1024,4]{1,0:T(8,128)S(1)} all-reduce(f32[1024,4]{1,0:T(8,128)S(1)} %copy.78), channel_id=3, replica_groups=mesh['item'=64,'dp'=4] {'item'}, use_global_device_ids=true, to_apply=%region_14.15.clone | all-reduce | flops 4096 | bytes 32768
  651.9 45.9 %all-reduce.8.cloned.1.call-done = (f32[256,512]{0,1:T(8,128)}, f32[512,256]{1,0:T(8,128)}) async-done(((f32[256,512]{0,1:T(8,128)}, f32[512,256]{1,0:T(8,128)}), (f32[256,512]{0,1:T(8,128)}, f32[512,256]{1,0:T(8,128)})) %all-reduce.8.cloned.1.call-update) | async-done | bytes 1048592 | tf_op jit(solution)/shard_map/psum | solution.py:142
  698.0 9.1 %psum.54 = f32[512,4]{0,1:T(4,128)S(1)} all-reduce(f32[512,4]{0,1:T(4,128)S(1)} %fusion.30), channel_id=1, replica_groups=mesh['item'=64,'dp'=4] {'dp'}, use_global_device_ids=true, to_apply=%region_19.20 | all-reduce | flops 2048 | bytes 16384 | tf_op jit(solution)/shard_map/psum | solution.py:142
  707.2 128.5 %psum.55 = f32[512,4]{0,1:T(4,128)} all-reduce(f32[512,4]{0,1:T(4,128)S(1)} %psum.54), channel_id=1, replica_groups=mesh['item'=64,'dp'=4] {'item'}, use_global_device_ids=true, to_apply=%region_20.21 | all-reduce | flops 2048 | bytes 16384 | tf_op jit(solution)/shard_map/psum | solution.py:141
  836.6 53.1 %all-reduce.6.cloned.1.call-done = (f32[256,512]{0,1:T(8,128)}, f32[512,256]{1,0:T(8,128)}) async-done(((f32[256,512]{0,1:T(8,128)}, f32[512,256]{1,0:T(8,128)}), (f32[256,512]{0,1:T(8,128)}, f32[512,256]{1,0:T(8,128)})) %all-reduce.6.cloned.1.call-update) | async-done | bytes 1048592 | tf_op jit(solution)/shard_map/psum | solution.py:141
  (165 shorter events, 69.8 us)
Async XLA Ops:
  7.2 7.3 copy-start
  7.2 639.9 %reduce-scatter.2.cloned.1.call-start = ((), (), s32[]{:S(2)}) async-start(), calls=%async_computation.1 | async-start | bytes 1064960 | tf_op jit(solution)/shard_map/reduce_scatter | solution.py:118
  10.2 3.6 copy-start.16
  10.2 4.2 copy-start.11
  10.2 5.0 copy-start.2
  16.3 0.6 copy-start.7
  73.4 13.9 %copy-start.18 = (bf16[512,4]{0,1:T(4,128)(2,1)S(1)}, bf16[512,4]{0,1:T(4,128)(2,1)}, u32[]{:S(2)}) copy-start(bf16[512,4]{0,1:T(4,128)(2,1)} %param.17) | copy-start | bytes 12292
  80.4 7.1 copy-start.10
  137.7 8.9 copy-start.5
  143.7 2.7 copy-start.15
  144.3 2.9 copy-start.4
  147.2 245.3 %copy-start.17 = (s32[1,64]{1,0:T(1,128)S(1)}, s32[1,64]{1,0:T(1,128)}, u32[]{:S(2)}) copy-start(s32[1,64]{1,0:T(1,128)} %param.12) | copy-start | bytes 772
  147.2 245.4 %copy-start.6 = (f32[1024,4]{0,1:T(4,128)S(1)}, f32[1024,4]{0,1:T(4,128)}, u32[]{:S(2)}) copy-start(f32[1024,4]{0,1:T(4,128)} %copy-done.5) | copy-start | bytes 49156
  149.4 4.4 copy-start.1
  163.9 4.4 copy-start.1
  178.8 4.4 copy-start.1
  193.6 4.4 copy-start.1
  208.4 4.4 copy-start.1
  223.3 4.4 copy-start.1
  238.1 4.4 copy-start.1
  252.9 4.4 copy-start.1
  265.6 130.7 %copy-start.9 = (f32[1,1024]{1,0:T(1,128)S(1)}, f32[1,1024]{1,0:T(1,128)}, u32[]{:S(2)}) copy-start(f32[1,1024]{1,0:T(1,128)} %and_select_fusion) | copy-start | bytes 12292
  265.6 130.9 %copy-start.14 = (f32[16,4]{1,0:T(8,128)S(1)}, f32[16,4]{1,0:T(8,128)}, u32[]{:S(2)}) copy-start(f32[16,4]{1,0:T(8,128)} %get-tuple-element.225) | copy-start | bytes 772
  265.7 131.1 %copy-start.20 = (u32[256]{0:T(256)S(1)}, u32[256]{0:T(256)}, u32[]{:S(2)}) copy-start(u32[256]{0:T(256)} %constant.108) | copy-start | bytes 3076
  265.7 382.5 %copy-start.8 = (f32[16,256]{1,0:T(8,128)S(1)}, f32[16,256]{1,0:T(8,128)}, u32[]{:S(2)}) copy-start(f32[16,256]{1,0:T(8,128)} %copy-done.7) | copy-start | bytes 49156
  265.7 383.3 %copy-start.3 = (bf16[512,256]{1,0:T(8,128)(2,1)S(1)}, bf16[512,256]{1,0:T(8,128)(2,1)}, u32[]{:S(2)}) copy-start(bf16[512,256]{1,0:T(8,128)(2,1)} %param.16) | copy-start | bytes 786436
  393.4 257.1 %copy-start.13 = (f32[16,512]{1,0:T(8,128)S(1)}, f32[16,512]{1,0:T(8,128)}, u32[]{:S(2)}) copy-start(f32[16,512]{1,0:T(8,128)} %get-tuple-element.228) | copy-start | bytes 98308
  393.4 257.1 %copy-start.19 = (bf16[512,4]{0,1:T(4,128)(2,1)S(1)}, bf16[512,4]{0,1:T(4,128)(2,1)}, u32[]{:S(2)}) copy-start(bf16[512,4]{0,1:T(4,128)(2,1)} %param.17) | copy-start | bytes 12292
  393.4 257.2 %copy-start.12 = (bf16[1,16,256]{2,1,0:T(8,128)(2,1)S(1)}, bf16[1,16,256]{2,1,0:T(8,128)(2,1)}, u32[]{:S(2)}) copy-start(bf16[1,16,256]{2,1,0:T(8,128)(2,1)} %param.10) | copy-start | bytes 24580
  396.2 301.5 %all-reduce.8.cloned.1.call-start = ((), (), s32[]{:S(2)}) async-start(), calls=%async_computation.3 | async-start | bytes 2097152 | tf_op jit(solution)/shard_map/psum | solution.py:142
  651.9 237.9 %all-reduce.6.cloned.1.call-start = ((), (), s32[]{:S(2)}) async-start(), calls=%async_computation.2 | async-start | bytes 2097152 | tf_op jit(solution)/shard_map/psum | solution.py:141
Sparse Core Ops, SparseCore 0:
  396.4 134.9 reduce-scatter.1
  652.0 45.7 all-reduce.7
  701.7 188.0 all-reduce.5
